TPU v7x, 32 devices: a whole 2x2x4 slice. The times are simulated.
32 devices in a mesh: gx: 4 (over z), gy: 4 (over y, core), gz: 2 (over x).
Axes of the slice: x: 2, y: 2, z: 4, core: 2. Of those that a mesh axis runs over, the one named last changes fastest.
Arguments:
- grads: float32 [4, 4, 2, 16, 14336], P('gx', 'gy', 'gz'), may hold values from -100 to 100
- plan: int32 [3], replicated, may hold values from 0 to 2, each once
Outputs:
- averaged: float32 [4, 4, 2, 16, 14336], P('gx', 'gy', 'gz')
- reports: float32 [3], replicated
Inputs may be any that keep to these rules, and one draw needn't show every extreme that they name: `plan`: each of 0, 1, 2 appears once.
All inputs are finite; a program needn't handle non-finite values.
Results may differ from a plain program's by a relative error of at most 0.0003.
Values sent between devices are 32-bit elements; how exact they have to be, the bound alone decides.
A program may use at most 64 MiB of HBM per device.

v0:
```python
import jax
import jax.numpy as jnp
from jax import lax
from jax.sharding import PartitionSpec as P


def report(deviation):
    return lax.pmax(deviation, ("gx", "gy", "gz"))


def settle(stacked):
    group = jnp.sum(stacked, axis=0) / stacked.shape[0]
    deviation = jnp.max(jnp.abs(stacked - group[None]))
    return (group, deviation)


def chain_gx(blocks):
    return settle(lax.all_to_all(blocks[None], "gx", split_axis=1, concat_axis=0, tiled=True))


def chain_gy(blocks):
    return settle(lax.all_to_all(blocks[None], "gy", split_axis=2, concat_axis=0, tiled=True))


def chain_gz(blocks):
    return settle(lax.all_to_all(blocks[None], "gz", split_axis=3, concat_axis=0, tiled=True))


def make_order(order):
    helpers = [chain_gx, chain_gy, chain_gz]

    def run(blocks):
        values = []
        for axis_id in order:
            blocks, deviation = helpers[axis_id](blocks)
            values.append(report(deviation))
        return (blocks.reshape(-1), jnp.stack(values).astype(jnp.float32))

    return run


def on_device(grads, plan):
    blocks = grads.reshape(lax.axis_size("gx"), lax.axis_size("gy"), lax.axis_size("gz"), -1)
    branches = []
    for first in range(3):
        for second in range(3):
            if first == second:
                branches.append(make_order((0, 1, 2)))
            else:
                branches.append(make_order((first, second, 3 - first - second)))
    piece, stacked = lax.switch(plan[0] * 3 + plan[1], branches, blocks)
    whole = lax.all_gather(piece, ("gx", "gy", "gz"), axis=0, tiled=True)
    current = whole.reshape(grads.shape)
    return (current, stacked)


def solution(mesh):
    placed = (P("gx", "gy", "gz", None, None), P())
    return jax.shard_map(
        on_device,
        mesh=mesh,
        in_specs=placed,
        out_specs=(P("gx", "gy", "gz", None, None), P()),
        check_vma=False,
    )
```

profile of v0, /device:TPU:0, one launch (start us, length us, event | category | flops | bytes accessed | tf_op | source)
XLA Modules:
  0.0 184.4 jit_solution(281091975552552300)
XLA Ops:
  0.6 1.3 fusion.63
  3.2 107.4 %conditional.1 = (f32[3]{0:T(128)S(1)}, f32[7168]{0:T(1024)}, f32[7168]{0:T(1024)S(1)}) conditional(s32[]{:T(128)} %bitcast.91, f32[1,1,1,16,14336]{4,3,2,1,0:T(8,128)} %param.11, f32[1,1,1,16,14336]{4,3,2,1,0:T(8,128)} %param.11, f32[1,1,1,16,14336]{4,3,2,1,0:T(8,128)} %param.11, ...), branch_computations={%region_0.0_spmd, %region_10.0_spmd, %region_20.0_spmd, %region_30... | conditional | flops 1490950 | bytes 13906072 | solution.py:51
  3.3 2.0 %broadcast_in_dim_reshape.19 = f32[1,4,4,2,7168]{4,3,2,0,1:T(2,128)S(1)} reshape(f32[1,1,1,16,14336]{4,3,2,1,0:T(8,128)} %param.1) | data formatting | bytes 1835008 | tf_op jit(solution)/shard_map/cond/branch_1_fun/broadcast_in_dim;reshape | solution.py:18
  5.2 29.1 %all_to_all.299 = f32[1,4,4,2,7168]{4,3,2,0,1:T(2,128)S(1)} all-to-all(f32[1,4,4,2,7168]{4,3,2,0,1:T(2,128)S(1)} %broadcast_in_dim_reshape.19), channel_id=1, replica_groups=mesh['gx'=4,'gy'=4,'gz'=2] {'gx'}, dimensions={1} | all-to-all | bytes 1835008 | tf_op jit(solution)/shard_map/cond/branch_1_fun/all_to_all | solution.py:18
  34.3 0.5 reduce_sum.219
  34.8 0.8 broadcast_multiply_fusion.2
  35.6 3.4 %all-to-all-start.4 = ((f32[1,1,4,2,7168]{4,3,1,0,2:T(2,128)}), f32[1,1,4,2,7168]{4,3,1,0,2:T(2,128)S(1)}, u32[]{:S(2)}, u32[]{:S(2)}) async-start(f32[1,1,4,2,7168]{4,3,1,0,2:T(2,128)} %get-tuple-element.50), calls=%async_computation.4 | async-start | bytes 458752 | tf_op jit(solution)/shard_map/cond/branch_1_fun/all_to_all | solution.py:22
  39.0 1.6 fusion.8
  40.6 4.0 %all-to-all-done.4 = f32[1,1,4,2,7168]{4,3,1,0,2:T(2,128)S(1)} async-done(((f32[1,1,4,2,7168]{4,3,1,0,2:T(2,128)}), f32[1,1,4,2,7168]{4,3,1,0,2:T(2,128)S(1)}, u32[]{:S(2)}, u32[]{:S(2)}) %all-to-all-start.4) | async-done | bytes 229408 | tf_op jit(solution)/shard_map/cond/branch_1_fun/all_to_all | solution.py:22
  44.6 0.1 reduce_sum.220
  44.8 0.7 div.70
  45.4 3.3 %all-to-all-start.5 = ((f32[1,1,1,2,7168]{4,2,1,0,3:T(1,128)}), f32[1,1,1,2,7168]{4,2,1,0,3:T(1,128)S(1)}, u32[]{:S(2)}, u32[]{:S(2)}) async-start(f32[1,1,1,2,7168]{4,2,1,0,3:T(1,128)} %div.70), calls=%async_computation.5 | async-start | bytes 114688 | tf_op jit(solution)/shard_map/cond/branch_1_fun/all_to_all | solution.py:26
  48.7 0.8 fusion.10
  49.6 3.2 %all-to-all-done.5 = f32[1,1,1,2,7168]{4,2,1,0,3:T(1,128)S(1)} async-done(((f32[1,1,1,2,7168]{4,2,1,0,3:T(1,128)}), f32[1,1,1,2,7168]{4,2,1,0,3:T(1,128)S(1)}, u32[]{:S(2)}, u32[]{:S(2)}) %all-to-all-start.5) | async-done | bytes 57376 | tf_op jit(solution)/shard_map/cond/branch_1_fun/all_to_all | solution.py:26
  52.8 0.1 reduce_sum.221
  52.9 0.0 copy-start.1
  52.9 0.6 copy-done.1
  53.5 0.8 fusion.12
  54.3 38.2 %all-reduce.1 = (f32[1]{0:T(128)}, f32[1]{0:T(128)}, f32[1]{0:T(128)}) all-reduce(f32[1]{0:T(128)} %bitcast.13, f32[1]{0:T(128)} %bitcast.11, f32[1]{0:T(128)} %bitcast.8), channel_id=1, replica_groups=mesh['gx'=4,'gy'=4,'gz'=2] {'gx','gy','gz'}, use_global_device_ids=true, to_apply=%region_19.0 | all-reduce | flops 3 | bytes 24 | tf_op jit(solution)/shard_map/cond/branch_1_fun/pmax | solution.py:8
  92.4 1.9 %pad_maximum_fusion.1 = f32[3]{0:T(128)S(1)} fusion(f32[1]{0:T(128)} %get-tuple-element.23, f32[1]{0:T(128)} %get-tuple-element.24, f32[1]{0:T(128)} %get-tuple-element.25), kind=kLoop, calls=%fused_computation.24 | loop fusion | flops 6 | bytes 24 | tf_op jit(solution)/shard_map/cond/branch_1_fun/stack | solution.py:37
  110.6 0.0 copy-start.9
  110.7 0.5 copy-done.9
  111.2 0.8 div.119
  111.9 70.9 %all_gather.3 = f32[229376]{0:T(1024)S(1)} all-gather(f32[7168]{0:T(1024)S(1)} %div.119), channel_id=1, replica_groups=mesh['gx'=4,'gy'=4,'gz'=2] {'gx','gy','gz'}, dimensions={0}, use_global_device_ids=true | all-gather | bytes 946176 | tf_op jit(solution)/shard_map/all_gather | solution.py:52
  182.8 1.1 reshape.1054
  (3 shorter events, 0.0 us)
Async XLA Ops:
  35.6 9.0 %all-to-all-start.4 = ((f32[1,1,4,2,7168]{4,3,1,0,2:T(2,128)}), f32[1,1,4,2,7168]{4,3,1,0,2:T(2,128)S(1)}, u32[]{:S(2)}, u32[]{:S(2)}) async-start(f32[1,1,4,2,7168]{4,3,1,0,2:T(2,128)} %get-tuple-element.50), calls=%async_computation.4 | async-start | bytes 458752 | tf_op jit(solution)/shard_map/cond/branch_1_fun/all_to_all | solution.py:22
  45.4 7.4 %all-to-all-start.5 = ((f32[1,1,1,2,7168]{4,2,1,0,3:T(1,128)}), f32[1,1,1,2,7168]{4,2,1,0,3:T(1,128)S(1)}, u32[]{:S(2)}, u32[]{:S(2)}) async-start(f32[1,1,1,2,7168]{4,2,1,0,3:T(1,128)} %div.70), calls=%async_computation.5 | async-start | bytes 114688 | tf_op jit(solution)/shard_map/cond/branch_1_fun/all_to_all | solution.py:26
  52.9 0.6 copy-start.1
  110.6 0.5 copy-start.9
where the time goes:
time: 187 us; the launch traced here: 184 us
  blocking collectives  138 us (74%)
  loops' own time  16.4 us (9%)
  other arithmetic  7.4 us (4%)
  waiting for transfers between devices  7.28 us (4%)
  starting transfers between devices  6.67 us (4%)
  local copies, waits for them, and re-layouts  6.1 us (3%)
  between operations  2.45 us (1%)
    all_gather x1, blocking collectives, on_device(): whole = lax.all_gather(piece, ('gx', 'gy', 'gz'), axis=0, tiled=True)  70.9 us
    pmax x1, blocking collectives, report(): return lax.pmax(deviation, ('gx', 'gy', 'gz'))  38.2 us
    all_to_all x1, blocking collectives, chain_gx(): lax.all_to_all(blocks[None], 'gx', split_axis=1, concat_axis=0, tiled=True)  29.1 us
    another operation x1, loops' own time, on_device(): piece, stacked = lax.switch(plan[0] * 3 + plan[1], branches, blocks)  16.4 us
    all_to_all x1, waiting for transfers between devices, chain_gy(): lax.all_to_all(blocks[None], 'gy', split_axis=2, concat_axis=0, tiled=True)  4.05 us
  transfers between devices with their start and end apart: 2, of which 2 were waited for; matrix products, arithmetic and copies ran while one was open for 1% of the time, Pallas kernels for 0%

commit v1 on v0

v1 whole, which is shorter than its diff:
```python
import functools
import itertools
import math

import jax
import jax.numpy as jnp
from jax import lax
from jax.experimental import pallas as pl
from jax.experimental.pallas import tpu as pltpu
from jax.sharding import PartitionSpec as P

AXES = ("gx", "gy", "gz")
LANES = 128
SUBLANES = 8
PLANS = {
    (0, 1, 2): (((0, 1, 2),), (3, 3, 1)),
    (0, 2, 1): (((0, 2, 1),), (3, 3, 1)),
    (1, 0, 2): (((1,), (0, 2)), (3, 2, 1, 1)),
    (1, 2, 0): (((1, 2), (0,)), (3, 2, 1, 1)),
    (2, 0, 1): (((2,), (0, 1)), (3, 2, 1, 1)),
    (2, 1, 0): (((2, 1), (0,)), (3, 2, 1, 1)),
}
FIRST_US = (20.0, 10.0, 10.0)
STEP_US = 3.0


def power_of_two(n):
    return n & (n - 1) == 0


def mean_of(total, n):
    return total * (1.0 / n) if power_of_two(n) else total / n


def chunks_of(p, shares):
    total, bounds, done = sum(shares), [0], 0
    for share in shares:
        done += share
        bounds.append(p * done // total)
    return [(lo, hi - lo) for lo, hi in zip(bounds[:-1], bounds[1:]) if hi > lo]


def gather_stages(sizes):
    if not power_of_two(sizes[1]):
        return [[(0, None)], [(2, None)], [(1, None)]]
    bits, bit = [], sizes[1] // 2
    while bit:
        bits.append((1, bit))
        bit //= 2
    return [[(0, None)], [(2, None)] + bits[:-1], bits[-1:]]


def gather_count(sizes):
    total, held = 0, [1, 1, 1]
    for stage in gather_stages(sizes):
        total += math.prod(held) * (math.prod(sizes[a] if bit is None else 2 for a, bit in stage) - 1)
        for axis, bit in stage:
            held[axis] = 1 if bit is None or bit == 1 else 2 * held[axis]
    return total


def offsets_of(axes, sizes):
    found = itertools.product(*[range(sizes[a]) if a in axes else (0,) for a in range(3)])
    return [d for d in sorted(found, key=lambda d: sum(min(i, n - i) for i, n in zip(d, sizes))) if any(d)]


class Copies:
    def __init__(self, send, recv):
        self.send, self.recv, self.count, self.all = send, recv, 0, []

    def start(self, src, dst, peer):
        copy = pltpu.make_async_remote_copy(
            src_ref=src,
            dst_ref=dst,
            send_sem=self.send.at[self.count],
            recv_sem=self.recv.at[self.count],
            device_id=tuple(peer),
            device_id_type=pl.DeviceIdType.MESH,
        )
        self.count += 1
        copy.start()
        self.all.append(copy)
        return copy


def kernel(order, sizes, p, x, out, reports, own, dev, rep, rep_recv, send_sem, recv_sem, own_sem, *bufs):
    groups, shares = PLANS[order]
    me = [lax.axis_index(name) for name in AXES]
    parts = chunks_of(p, shares)
    recvs = bufs[: len(groups)]
    curs = (own,) + bufs[len(groups) :]
    stages = gather_stages(sizes)
    rep_groups = ((0,), (1, 2))

    def peer_at(d):
        return [lax.rem(me[a] + d[a], sizes[a]) if d[a] else me[a] for a in range(3)]

    barrier = pltpu.get_barrier_semaphore()
    near = [set(group) for group in groups] + [set(group) for group in rep_groups]
    near += [{axis for axis, _ in stage} for stage in stages]
    greeted = [d for d in offsets_of((0, 1, 2), sizes) if any({a for a in range(3) if d[a]} <= axes for axes in near)]
    for d in greeted:
        pl.semaphore_signal(barrier, inc=1, device_id=tuple(peer_at(d)), device_id_type=pl.DeviceIdType.MESH)

    owns = []
    for k, (lo, size) in enumerate(parts):
        index = [me[a] if a in groups[0] else slice(None) for a in range(3)]
        rest = (slice(None),) * (3 - len(groups[0]))
        copy = pltpu.make_async_copy(x.at[(*index, pl.ds(lo, size))], own.at[(*rest, pl.ds(lo, size))], own_sem.at[k])
        copy.start()
        owns.append(copy)
    dev[...] = jnp.zeros_like(dev)
    pl.semaphore_wait(barrier, len(greeted))

    copies = Copies(send_sem, recv_sem)
    waiting = {}

    def left_at(g):
        return sorted(a for group in groups[g:] for a in group)

    def scatter(g, k):
        span = pl.ds(*parts[k])
        source = x if g == 0 else curs[g]
        left, rest = left_at(g), left_at(g + 1)
        waiting[g, k] = []
        for slot, d in enumerate(offsets_of(groups[g], sizes)):
            peer = peer_at(d)
            index = tuple(peer[a] if a in groups[g] else slice(None) for a in left)
            place = recvs[g].at[(slot, *[slice(None)] * len(rest), span)]
            waiting[g, k].append(copies.start(source.at[(*index, span)], place, peer))

    def settle(g, k):
        for copy in waiting[g, k]:
            copy.wait_recv()
        if g == 0:
            owns[k].wait()
        lo, size = parts[k]
        left, rest = left_at(g), left_at(g + 1)
        first = sum(len(group) for group in groups[:g])
        worst = {}
        for place in itertools.product(*[range(sizes[a]) for a in rest]):
            for t in range(lo, lo + size):
                where = dict(zip(rest, place))
                if g == 0:
                    mine = own[(*place, t)]
                else:
                    mine = curs[g][(*[where.get(a, me[a]) for a in left], t)]
                values = {(0, 0, 0): mine}
                for slot, d in enumerate(offsets_of(groups[g], sizes)):
                    values[d] = recvs[g][(slot, *place, t)]
                for r, axis in enumerate(groups[g], first):
                    members = {}
                    for d, value in values.items():
                        members.setdefault((*d[:axis], 0, *d[axis + 1 :]), []).append(value)
                    values = {}
                    for d, group in members.items():
                        mean = mean_of(functools.reduce(jnp.add, group), len(group))
                        values[d] = mean
                        for value in group:
                            gap = jnp.abs(value - mean)
                            worst[r] = jnp.maximum(worst[r], gap) if r in worst else gap
                (mean,) = values.values()
                if g == len(groups) - 1:
                    out[(me[0], me[1], me[2], t)] = mean
                else:
                    curs[g + 1][(*place, t)] = mean
        for r, gap in worst.items():
            dev[r] = jnp.maximum(dev[r], gap)

    held = {}

    def gather(k, s):
        span = pl.ds(*parts[k])
        if s == 0:
            held[k] = [[me[0]], [me[1]], [me[2]]]
        have = held[k]
        blocks = list(itertools.product(*[[slice(None)] if h is None else h for h in have]))
        choices = []
        for axis, bit in stages[s]:
            if bit is None:
                n = sizes[axis]
                choices.append([(axis, me[axis])] + [(axis, lax.rem(me[axis] + d, n)) for d in range(1, n)])
            else:
                choices.append([(axis, bit, 0), (axis, bit, 1)])
        waiting["gather", k] = []
        for number, choice in enumerate(itertools.product(*choices)):
            if number == 0:
                continue
            peer = list(me)
            flips = 0
            for part in choice:
                if len(part) == 2:
                    peer[part[0]] = part[1]
                elif part[2]:
                    high = lax.rem(me[part[0]] // part[1], 2)
                    flips = flips + part[1] - 2 * part[1] * high
                    peer[part[0]] = me[part[0]] + flips
            for block in blocks:
                piece = out.at[(*block, span)]
                waiting["gather", k].append(copies.start(piece, piece, peer))
        for axis, bit in stages[s]:
            if bit is None or bit == 1:
                have[axis] = None
            else:
                turn = bit - 2 * bit * lax.rem(me[axis] // bit, 2)
                have[axis] = have[axis] + [i + turn for i in have[axis]]

    def landed(k):
        for copy in waiting["gather", k]:
            copy.wait_recv()

    def tell(s):
        base = sum(len(offsets_of(group, sizes)) for group in rep_groups[:s])
        if s == 0:
            rows = lax.broadcasted_iota(jnp.int32, (SUBLANES, LANES), 0)
            tile = jnp.zeros((SUBLANES, LANES), jnp.float32)
            for r in range(3):
                tile = jnp.where(rows == r, jnp.max(dev[r]), tile)
            rep[0] = tile
        waiting["rep", s] = []
        for slot, d in enumerate(offsets_of(rep_groups[s], sizes), base):
            waiting["rep", s].append(copies.start(rep.at[s], rep_recv.at[slot], peer_at(d)))

    def told(s):
        base = sum(len(offsets_of(group, sizes)) for group in rep_groups[:s])
        for copy in waiting["rep", s]:
            copy.wait_recv()
        tile = rep[s]
        for slot in range(base, base + len(waiting["rep", s])):
            tile = jnp.maximum(tile, rep_recv[slot])
        if s == 0:
            rep[1] = tile
        else:
            for r in range(3):
                reports[r] = jnp.max(tile[r : r + 1])

    for k in range(len(parts)):
        scatter(0, k)

    events = []
    whole = FIRST_US[order[0]]
    for k, (lo, size) in enumerate(parts):
        at = whole * (lo + size) / p

        def reduce_step(g, k):
            settle(g, k)
            if g + 1 < len(groups):
                scatter(g + 1, k)
            else:
                gather(k, 0)

        for g in range(len(groups)):
            events.append((at + g * STEP_US, k, functools.partial(reduce_step, g, k)))
        if order[0] == 0:
            at = whole
        at += (len(groups) - 1) * STEP_US

        def gather_step(k, s):
            landed(k)
            if s < len(stages):
                gather(k, s)

        for s in range(1, len(stages) + 1):
            events.append((at + s * STEP_US, k, functools.partial(gather_step, k, s)))
        if k == len(parts) - 1:

            def rep_step(s):
                if s:
                    told(s - 1)
                if s < 2:
                    tell(s)

            for s in range(3):
                events.append((at + s * STEP_US + 0.1, k, functools.partial(rep_step, s)))
    for _, _, step in sorted(events, key=lambda event: event[:2]):
        step()
    for copy in copies.all:
        copy.wait_send()


def run(which, order, sizes, p, x):
    tile = (SUBLANES, LANES)
    f32 = jnp.float32
    groups, shares = PLANS[order]
    parts = len(chunks_of(p, shares))
    reps = len(offsets_of((0,), sizes)) + len(offsets_of((1, 2), sizes))
    copies = reps + parts * sum(len(offsets_of(group, sizes)) for group in groups)
    copies += parts * gather_count(sizes)
    recvs, curs = [], []
    for g, group in enumerate(groups):
        rest = [sizes[a] for a in sorted(a for later in groups[g + 1 :] for a in later)]
        recvs.append(pltpu.VMEM((len(offsets_of(group, sizes)), *rest, p, *tile), f32))
        if g == 0:
            own = pltpu.VMEM((*rest, p, *tile), f32)
        if g + 1 < len(groups):
            curs.append(pltpu.VMEM((*rest, p, *tile), f32))
    scratch = [own, pltpu.VMEM((3, *tile), f32), pltpu.VMEM((2, *tile), f32), pltpu.VMEM((reps, *tile), f32)]
    scratch += [pltpu.SemaphoreType.DMA((copies,)), pltpu.SemaphoreType.DMA((copies,)), pltpu.SemaphoreType.DMA((parts,))]
    return pl.pallas_call(
        functools.partial(kernel, order, sizes, p),
        out_shape=(jax.ShapeDtypeStruct(x.shape, f32), jax.ShapeDtypeStruct((3,), f32)),
        in_specs=[pl.BlockSpec(memory_space=pl.ANY)],
        out_specs=(pl.BlockSpec(memory_space=pltpu.VMEM), pl.BlockSpec(memory_space=pltpu.SMEM)),
        scratch_shapes=scratch + recvs + curs,
        compiler_params=pltpu.CompilerParams(collective_id=which, has_side_effects=True),
        name=f"moshpit_{which}",
    )(x)


def on_device(sizes, grads, plan):
    rows, columns = grads.shape[-2:]
    high, wide = rows // SUBLANES, columns // LANES
    tiles = high * wide
    p = -(-tiles // math.prod(sizes))
    x = grads.reshape(high, SUBLANES, wide, LANES).transpose(0, 2, 1, 3).reshape(tiles, SUBLANES, LANES)
    spare = p * math.prod(sizes) - tiles
    if spare:
        x = jnp.pad(x, ((0, spare), (0, 0), (0, 0)))
    x = x.reshape(*sizes, p, SUBLANES, LANES)
    orders = [(0, 1, 2), (0, 2, 1), (1, 0, 2), (1, 2, 0), (1, 2, 0), (2, 0, 1), (2, 1, 0)]
    names = {order: i for i, order in enumerate(PLANS)}
    branches = [functools.partial(run, names[order], order, sizes, p) for order in orders]
    place = lax.iota(jnp.int32, 3)
    choice = jnp.sum(plan * ((3 - place) * (2 - place) // 2)) - 1
    out, reports = lax.switch(choice, branches, x)
    out = out.reshape(-1, SUBLANES, LANES)[:tiles]
    out = out.reshape(high, wide, SUBLANES, LANES).transpose(0, 2, 1, 3).reshape(grads.shape)
    return out, reports


def solution(mesh):
    sizes = tuple(mesh.shape[name] for name in AXES)
    placed = (P("gx", "gy", "gz", None, None), P())
    return jax.shard_map(
        functools.partial(on_device, sizes), mesh=mesh, in_specs=placed, out_specs=placed, check_vma=False
    )
```

time: 187 us -> 40.7 us (0.22); the launches traced: 184 us -> 40.6 us
  blocking collectives: 138 us -> 0 us
  Pallas kernels: 0 us -> 36.5 us
  loops' own time: 16.4 us -> 0.05 us
  waiting for transfers between devices: 7.28 us -> 0 us
  starting transfers between devices: 6.67 us -> 0 us
  other arithmetic: 7.4 us -> 1.3 us
  local copies, waits for them, and re-layouts: 6.1 us -> 1.44 us
    all_gather x1 -> x0, blocking collectives: 70.9 us -> none  [on_device(): whole = lax.all_gather(piece, ('gx', 'gy', 'gz'), axis=0, tiled=True)]
    pmax x1 -> x0, blocking collectives: 38.2 us -> none  [report(): return lax.pmax(deviation, ('gx', 'gy', 'gz'))]
    pallas_call x0 -> x1, Pallas kernels: none -> 36.5 us  [run(): pl.pallas_call(functools.partial(kernel, order, sizes, p), out_shape=(jax...]
    all_to_all x1 -> x0, blocking collectives: 29.1 us -> none  [chain_gx(): lax.all_to_all(blocks[None], 'gx', split_axis=1, concat_axis=0, tiled=True)]
    another operation x1, loops' own time: 16.4 us -> 0.05 us  [on_device(): out, reports = lax.switch(choice, branches, x)]
    all_to_all x2 -> x0, waiting for transfers between devices: 7.28 us -> none  [the longest x1 4.05 us: chain_gy(): lax.all_to_all(blocks[None], 'gy', split_axis=2, concat_axis=0, tiled=True)]
    all_to_all x2 -> x0, starting transfers between devices: 6.67 us -> none  [the longest x1 3.39 us: chain_gy(): lax.all_to_all(blocks[None], 'gy', split_axis=2, concat_axis=0, tiled=True)]
    reduce_max x3 -> x0, other arithmetic: 3.2 us -> none  [settle(): deviation = jnp.max(jnp.abs(stacked - group[None]))]
  transfers between devices with their start and end apart: 2 -> 0, of which waited for: 2 -> 0; matrix products, arithmetic and copies ran while one was open for 1% -> 0% of each run, Pallas kernels for 0% -> 0%
where the time goes in v1:
time: 40.7 us; the launch traced here: 40.6 us
  Pallas kernels  36.5 us (90%)
  local copies, waits for them, and re-layouts  1.44 us (4%)
  other arithmetic  1.3 us (3%)
  between operations  1.29 us (3%)
    pallas_call x1, Pallas kernels, run(): pl.pallas_call(functools.partial(kernel, order, sizes, p), out_shape=(jax...  36.5 us
    unnamed x2, local copies, waits for them, and re-layouts  1.44 us
    reduce_sum x1, other arithmetic, on_device(): choice = jnp.sum(plan * ((3 - place) * (2 - place) // 2)) - 1  1.3 us

profile of v1, /device:TPU:0, one launch (start us, length us, event | category | flops | bytes accessed | tf_op | source)
XLA Modules:
  0.0 40.6 jit_solution(10891247713064493695)
XLA Ops:
  0.6 1.3 %multiply_reduce_fusion = s32[]{:T(128)} fusion(s32[3]{0:T(128)} %param.10), kind=kLoop, calls=%fused_computation.7 | loop fusion | flops 59 | bytes 16 | tf_op jit(solution)/shard_map/reduce_sum | solution.py:324
  2.6 36.5 %conditional.1 = ((f32[4,4,2,7,8,128]{5,4,3,2,1,0:T(8,128)S(1)}, f32[3]{0:T(128)S(1)})) conditional(s32[]{:T(128)} %clamp.3, f32[4,4,2,7,8,128]{5,4,3,2,1,0:T(8,128)} %bitcast.10, f32[4,4,2,7,8,128]{5,4,3,2,1,0:T(8,128)} %bitcast.11, f32[4,4,2,7,8,128]{5,4,3,2,1,0:T(8,128)} %bitcast.12, ...), branch_computations={%region_1.2_spmd, %region_2.3_spmd, %region_3.4_spmd, %region_4.5_... | conditional | bytes 8 | solution.py:325
  2.6 36.5 %moshpit_4.1 = (f32[4,4,2,7,8,128]{5,4,3,2,1,0:T(8,128)S(1)}, f32[3]{0:T(128)S(1)}) custom-call(f32[4,4,2,7,8,128]{5,4,3,2,1,0:T(8,128)} %x.5), custom_call_target="tpu_custom_call" | custom-call | tf_op jit(solution)/shard_map/cond/branch_5_fun/moshpit_4/pallas_call | solution.py:299
  39.1 0.9 %copy.20 = f32[1,1,1,16,14336]{4,3,2,1,0:T(8,128)} copy(f32[1,1,1,16,14336]{4,3,2,1,0:T(8,128)S(1)} %bitcast.17) | data formatting | bytes 1835008
  40.1 0.5 %copy.21 = f32[3]{0:T(128)} copy(f32[3]{0:T(128)S(1)} %get-tuple-element.30) | data formatting | bytes 24
